TPU v7x, 32 devices: a whole 2x2x4 slice. The times are simulated.
32 devices in a mesh: walker: 2 (over core), slab: 2 (over x), chol: 8 (over z, y).
Axes of the slice: x: 2, y: 2, z: 4, core: 2. Of those that a mesh axis runs over, the one named last changes fastest.
Arguments:
- cholesky_factors: bfloat16 [96, 256, 2048], P('chol', None, 'slab'), may hold values from -0.13183594 to 0.13183594
- greens: bfloat16 [2, 256, 2048], P('walker', 'chol', 'slab'), may hold values from -1.7265625 to 1.7265625
- walker_weights: float32 [2], P('walker'), may hold values from 0.3 to 3
Outputs:
- fock: float32 [256, 2048], P(('walker', 'chol'), 'slab')
All inputs are finite; a program needn't handle non-finite values.
Results may differ from a plain program's by a relative error of at most 0.0029.
Values may be sent and summed in bfloat16 or wider, within the bound.
A program may use at most 64 MiB of HBM per device.

v0:
```python
import jax
import jax.numpy as jnp
from jax import lax
from jax.sharding import PartitionSpec as P


def per_device(cholesky_factors, greens, walker_weights):
    theta = greens[0]
    weight = walker_weights[0]
    panel_sum_terms = jnp.einsum(
        "gnp,mp->gnm",
        cholesky_factors,
        lax.all_gather(theta, "chol", axis=0, tiled=True),
        preferred_element_type=jnp.float32,
    )
    margin = lax.psum(panel_sum_terms, "slab").astype(jnp.bfloat16)
    terms = jnp.einsum("gnm,gmp->np", margin, cholesky_factors, preferred_element_type=jnp.float32)
    weighted = weight * terms
    return lax.psum_scatter(weighted, ("walker", "chol"), scatter_dimension=0, tiled=True)


def solution(mesh):
    in_specs = (P("chol", None, "slab"), P("walker", "chol", "slab"), P("walker"))
    out_specs = P(("walker", "chol"), "slab")
    return jax.shard_map(
        per_device, mesh=mesh, in_specs=in_specs, out_specs=out_specs, check_vma=False
    )
```

profile of v0, /device:TPU:0, one launch (start us, length us, event | category | flops | bytes accessed | tf_op | source)
XLA Modules:
  0.0 186.0 jit_solution(11552046378946766272)
XLA Ops:
  6.5 0.0 reduce-scatter.2.cloned.1.call-start
  6.5 33.2 %all-gather = bf16[1,256,1024]{2,1,0:T(8,128)(2,1)S(1)} all-gather(bf16[1,32,1024]{2,1,0:T(8,128)(2,1)} %param.4), channel_id=2, replica_groups=mesh['walker'=2,'slab'=2,'chol'=8] {'chol'}, dimensions={1}, use_global_device_ids=true | all-gather | bytes 589824 | tf_op jit(solution)/shard_map/all_gather | solution.py:13
  39.8 4.6 %fusion.8 = f32[12,256,256]{2,1,0:T(8,128)S(1)} fusion(bf16[12,256,1024]{2,1,0:T(8,128)(2,1)} %param.3, bf16[1,256,1024]{2,1,0:T(8,128)(2,1)S(1)} %all-gather), kind=kOutput, calls=%fused_computation.4 | convolution fusion | flops 1610612736 | bytes 9961472 | tf_op jit(solution)/shard_map/gnp,mp->gnm/dot_general | solution.py:10
  44.4 69.8 %all-reduce.1 = bf16[12,256,256]{2,1,0:T(8,128)(2,1)} all-reduce(f32[12,256,256]{2,1,0:T(8,128)S(1)} %fusion.8), channel_id=1, replica_groups=mesh['walker'=2,'slab'=2,'chol'=8] {'slab'}, use_global_device_ids=true, to_apply=%region_0.0 | all-reduce | flops 786432 | bytes 4718592 | tf_op jit(solution)/shard_map/psum | solution.py:16
  114.8 6.0 %fusion.5 = f32[256,1024]{1,0:T(8,128)} fusion(bf16[12,256,1024]{2,1,0:T(8,128)(2,1)} %param.3, bf16[12,256,256]{2,1,0:T(8,128)(2,1)} %all-reduce.1, f32[]{:T(128)} %bitcast.12), kind=kOutput, calls=%fused_computation.3 | convolution fusion | flops 1610874880 | bytes 8912900 | tf_op jit(solution)/shard_map/gnm,gmp->np/dot_general | solution.py:17
  120.9 0.0 reduce-scatter.2.cloned.1.call-update
  120.9 58.2 %reduce-scatter.2.cloned.1.call-done = f32[16,1024]{1,0:T(8,128)} async-done(((f32[256,1024]{1,0:T(8,128)}), f32[16,1024]{1,0:T(8,128)}) %reduce-scatter.2.cloned.1.call-update) | async-done | bytes 65552 | tf_op jit(solution)/shard_map/reduce_scatter | solution.py:19
Async XLA Ops:
  6.5 172.6 %reduce-scatter.2.cloned.1.call-start = ((), (), s32[]{:S(2)}) async-start(), calls=%async_computation.1 | async-start | bytes 1114112 | tf_op jit(solution)/shard_map/reduce_scatter | solution.py:19
Sparse Core Ops, SparseCore 0:
  121.0 58.0 reduce-scatter.1
where the time goes:
time: 186 us
  blocking collectives  103 us (55%)
  waiting for transfers between devices  58.3 us (31%)
  between operations  14 us (8%)
  matrix products  10.6 us (6%)
    psum x1, blocking collectives, per_device(): margin = lax.psum(panel_sum_terms, 'slab').astype(jnp.bfloat16)  69.8 us
    reduce_scatter x1, waiting for transfers between devices, per_device(): lax.psum_scatter(weighted, ('walker', 'chol'), scatter_dimension=0, tiled...  58.2 us
    all_gather x1, blocking collectives, per_device(): lax.all_gather(theta, 'chol', axis=0, tiled=True)  33.2 us
    dot_general x1, matrix products, per_device(): jnp.einsum('gnm,gmp->np', margin, cholesky_factors, preferred_element_typ...  6.03 us
    dot_general x1, matrix products, per_device(): jnp.einsum('gnp,mp->gnm', cholesky_factors, lax.all_gather(theta, 'chol',...  4.62 us
  transfers between devices with their start and end apart: 1, of which 1 were waited for; matrix products, arithmetic and copies ran while one was open for 0% of the time, Pallas kernels for 0%

commit v1 on v0

v1 whole, which is shorter than its diff:
```python
import functools

import jax
import jax.numpy as jnp
from jax import lax
from jax.experimental import pallas as pl
from jax.experimental.pallas import tpu as pltpu
from jax.sharding import PartitionSpec as P

MESH = pl.DeviceIdType.MESH
NT = (((1,), (1,)), ((), ()))


def exchange_kernel(
    sizes, l_hbm, theta_ref, weight_ref, out_ref,
    lv, th, wbuf, own, sbuf, rbuf, fsend, frecv,
    l_sem, w_sem, z_send, y_send, c_send, th_recv, x_send, x_recv, f_send, f_recv,
):
    n_chol, vectors, occupied, block_rows = sizes
    n_hi = n_chol // 2
    half = occupied // 2
    chunk_rows = 2 * block_rows
    n_chunks = n_hi
    w = lax.axis_index("walker")
    s = lax.axis_index("slab")
    me = lax.axis_index("chol")
    z, y = me // 2, me % 2
    sibling = {"walker": 1 - w}
    peer = {"slab": 1 - s}
    y_peer = {"chol": z * 2 + 1 - y}

    mine = pl.ds(pl.multiple_of(w * half, half), half)
    other = pl.ds(pl.multiple_of((1 - w) * half, half), half)
    load_mine = pltpu.make_async_copy(l_hbm.at[:, mine], lv.at[:, mine], l_sem.at[0])
    load_other = pltpu.make_async_copy(l_hbm.at[:, other], lv.at[:, other], l_sem.at[1])
    load_mine.start()
    load_other.start()
    wbuf[w] = jnp.full(wbuf.shape[1:], weight_ref[0], jnp.float32)

    barrier = pltpu.get_barrier_semaphore()
    for k in range(1, n_chol):
        pl.semaphore_signal(
            barrier, inc=1, device_id={"chol": lax.rem(me + k, n_chol)}, device_id_type=MESH
        )
    pl.semaphore_signal(barrier, inc=1, device_id=sibling, device_id_type=MESH)
    pl.semaphore_signal(barrier, inc=1, device_id=peer, device_id_type=MESH)
    pl.semaphore_wait(barrier, n_chol + 1)

    def rdma(src, dst, send, recv, to):
        return pltpu.make_async_remote_copy(
            src_ref=src, dst_ref=dst, send_sem=send, recv_sem=recv, device_id=to, device_id_type=MESH
        )

    sends = []

    def send(src, block, sem, to):
        copy = rdma(src, th.at[w, block], sem, th_recv.at[w, block], to)
        copy.start()
        sends.append(copy)

    def arrived(walker, block):
        rdma(th.at[walker, block], th.at[walker, block], c_send.at[0], th_recv.at[walker, block], sibling).wait_recv()

    first = theta_ref.at[0]
    send(first, me, y_send.at[0], y_peer)
    order = sorted(range(1, n_hi), key=lambda d: min(d, n_hi - d))
    for d in order:
        send(first, me, z_send.at[d], {"chol": lax.rem(z + d, n_hi) * 2 + y})
    send(first, me, c_send.at[0], sibling)
    weights = rdma(wbuf.at[w], wbuf.at[w], w_sem.at[0], w_sem.at[1], sibling)
    weights.start()
    th[w, me] = theta_ref[0]
    count = 1
    for i, d in enumerate(order):
        block = lax.rem(z + n_hi - d, n_hi) * 2 + y
        arrived(w, block)
        send(th.at[w, block], block, y_send.at[1 + i], y_peer)
        send(th.at[w, block], block, c_send.at[count], sibling)
        count += 1
    for d in [0] + order:
        block = lax.rem(z + n_hi - d, n_hi) * 2 + 1 - y
        arrived(w, block)
        send(th.at[w, block], block, c_send.at[count], sibling)
        count += 1
    for block in range(n_chol):
        arrived(1 - w, block)
    rdma(wbuf.at[1 - w], wbuf.at[1 - w], w_sem.at[0], w_sem.at[1], sibling).wait_recv()
    load_mine.wait()

    def margins(t, carry):
        at = lax.rem(z + 1 + t, n_hi)
        rows = pl.ds(pl.multiple_of(w * half + at * chunk_rows, chunk_rows), chunk_rows)
        x = lv[:, rows, :].reshape(vectors * chunk_rows, -1)
        a = 0.0
        for k in range(2):
            part = lax.dot_general(
                x, th[k].reshape(occupied, -1), NT, preferred_element_type=jnp.float32
            )
            a = a + wbuf[k][:1, :1] * part
        own[t] = a
        sbuf[t] = a.astype(jnp.bfloat16)
        rdma(sbuf.at[t], rbuf.at[t], x_send.at[t], x_recv.at[t], peer).start()
        return carry

    lax.fori_loop(0, n_chunks, margins, 0)
    load_other.wait()

    def fock(t, carry):
        at = lax.rem(z + 1 + t, n_hi)
        rdma(sbuf.at[t], rbuf.at[t], x_send.at[t], x_recv.at[t], peer).wait_recv()
        total = own[t] + rbuf[t].astype(jnp.float32)
        total = jnp.concatenate(
            [total[g * chunk_rows : (g + 1) * chunk_rows] for g in range(vectors)], axis=1
        )
        high = total.astype(jnp.bfloat16)
        low = (total - high.astype(jnp.float32)).astype(jnp.bfloat16)
        both = jnp.dot(
            jnp.concatenate([high, low], axis=0),
            lv[...].reshape(vectors * occupied, -1),
            preferred_element_type=jnp.float32,
        )
        f = both[:chunk_rows] + both[chunk_rows:]
        for d in range(2):
            fsend[t, d] = f[d * block_rows : (d + 1) * block_rows]
            to = at * 2 + d

            @pl.when(to != me)
            def _():
                rdma(fsend.at[t, d], frecv.at[me], f_send.at[t, d], f_recv.at[me], {"chol": to}).start()

        return carry

    lax.fori_loop(0, n_chunks, fock, 0)

    result = fsend[n_chunks - 1, y]
    for k in range(1, n_chol):
        source = lax.rem(me + k, n_chol)
        rdma(frecv.at[source], frecv.at[source], f_send.at[0, 0], f_recv.at[source], sibling).wait_recv()
        result = result + frecv[source]
    out_ref[...] = result

    for copy in sends:
        copy.wait_send()
    weights.wait_send()

    def drain(t, carry):
        at = lax.rem(z + 1 + t, n_hi)
        rdma(sbuf.at[t], rbuf.at[t], x_send.at[t], x_recv.at[t], peer).wait_send()
        for d in range(2):

            @pl.when(at * 2 + d != me)
            def _():
                rdma(fsend.at[t, d], frecv.at[me], f_send.at[t, d], f_recv.at[me], peer).wait_send()

        return carry

    lax.fori_loop(0, n_chunks, drain, 0)


def fused(n_chol, cholesky_factors, greens, walker_weights):
    vectors, occupied, orbitals = cholesky_factors.shape
    theta_rows = greens.shape[1]
    block_rows = occupied // (2 * n_chol)
    n_hi = n_chol // 2
    rows = vectors * 2 * block_rows
    dma = pltpu.SemaphoreType.DMA
    return pl.pallas_call(
        functools.partial(exchange_kernel, (n_chol, vectors, occupied, block_rows)),
        out_shape=jax.ShapeDtypeStruct((block_rows, orbitals), jnp.float32),
        in_specs=[
            pl.BlockSpec(memory_space=pl.ANY),
            pl.BlockSpec(memory_space=pltpu.VMEM),
            pl.BlockSpec(memory_space=pltpu.SMEM),
        ],
        out_specs=pl.BlockSpec(memory_space=pltpu.VMEM),
        scratch_shapes=[
            pltpu.VMEM((vectors, occupied, orbitals), jnp.bfloat16),
            pltpu.VMEM((2, n_chol, theta_rows, orbitals), jnp.bfloat16),
            pltpu.VMEM((2, 8, 128), jnp.float32),
            pltpu.VMEM((n_hi, rows, occupied), jnp.float32),
            pltpu.VMEM((n_hi, rows, occupied), jnp.bfloat16),
            pltpu.VMEM((n_hi, rows, occupied), jnp.bfloat16),
            pltpu.VMEM((n_hi, 2, block_rows, orbitals), jnp.float32),
            pltpu.VMEM((n_chol, block_rows, orbitals), jnp.float32),
            dma((2,)),
            dma((2,)),
            dma((n_hi,)),
            dma((n_hi,)),
            dma((n_chol,)),
            dma((2, n_chol)),
            dma((n_hi,)),
            dma((n_hi,)),
            dma((n_hi, 2)),
            dma((n_chol,)),
        ],
        compiler_params=pltpu.CompilerParams(collective_id=0, has_side_effects=True),
    )(cholesky_factors, greens, walker_weights)


def plain(cholesky_factors, greens, walker_weights):
    panel_sum_terms = jnp.einsum(
        "gnp,mp->gnm",
        cholesky_factors,
        lax.all_gather(greens[0], "chol", axis=0, tiled=True),
        preferred_element_type=jnp.float32,
    )
    margin = lax.psum(panel_sum_terms, "slab").astype(jnp.bfloat16)
    terms = jnp.einsum("gnm,gmp->np", margin, cholesky_factors, preferred_element_type=jnp.float32)
    weighted = walker_weights[0] * terms
    return lax.psum_scatter(weighted, ("walker", "chol"), scatter_dimension=0, tiled=True)


def solution(mesh):
    walkers, slabs, n_chol = (mesh.shape[axis] for axis in ("walker", "slab", "chol"))

    def per_device(cholesky_factors, greens, walker_weights):
        occupied = cholesky_factors.shape[1]
        pair = walkers == 2 and slabs == 2 and greens.shape[0] == 1
        if pair and n_chol % 2 == 0 and occupied % (16 * n_chol) == 0:
            return fused(n_chol, cholesky_factors, greens, walker_weights)
        return plain(cholesky_factors, greens, walker_weights)

    in_specs = (P("chol", None, "slab"), P("walker", "chol", "slab"), P("walker"))
    out_specs = P(("walker", "chol"), "slab")
    return jax.shard_map(
        per_device, mesh=mesh, in_specs=in_specs, out_specs=out_specs, check_vma=False
    )
```

time: 186 us -> 45.3 us (0.24)
  blocking collectives: 103 us -> 0 us
  waiting for transfers between devices: 58.3 us -> 0 us
  Pallas kernels: 0 us -> 42.9 us
  between operations: 14 us -> 0.66 us
  matrix products: 10.6 us -> 0 us
    psum x1 -> x0, blocking collectives: 69.8 us -> none  [per_device(): margin = lax.psum(panel_sum_terms, 'slab').astype(jnp.bfloat16)]
    reduce_scatter x1 -> x0, waiting for transfers between devices: 58.2 us -> none  [per_device(): lax.psum_scatter(weighted, ('walker', 'chol'), scatter_dimension=0, tiled...]
    pallas_call x0 -> x1, Pallas kernels: none -> 42.9 us  [fused(): pl.pallas_call(functools.partial(exchange_kernel, (n_chol, vectors, occup...]
    all_gather x1 -> x0, blocking collectives: 33.2 us -> none  [per_device(): lax.all_gather(theta, 'chol', axis=0, tiled=True)]
    dot_general x2 -> x0, matrix products: 10.6 us -> none  [the longest x1 6.03 us: per_device(): jnp.einsum('gnm,gmp->np', margin, cholesky_factors, preferred_element_typ...]
  transfers between devices with their start and end apart: 1 -> 0, of which waited for: 1 -> 0; matrix products, arithmetic and copies ran while one was open for 0% -> 0% of each run, Pallas kernels for 0% -> 0%
where the time goes in v1:
time: 45.3 us; the launch traced here: 45.1 us
  Pallas kernels  42.9 us (95%)
  local copies, waits for them, and re-layouts  1.47 us (3%)
  between operations  0.66 us (1%)
    pallas_call x1, Pallas kernels, fused(): pl.pallas_call(functools.partial(exchange_kernel, (n_chol, vectors, occup...  42.9 us
    unnamed x1, local copies, waits for them, and re-layouts  1.47 us

profile of v1, /device:TPU:0, one launch (start us, length us, event | category | flops | bytes accessed | tf_op | source)
XLA Modules:
  0.0 45.1 jit_solution(11515689532581079632)
XLA Ops:
  0.7 42.9 %shard_map.37 = f32[16,1024]{1,0:T(8,128)} custom-call(bf16[12,256,1024]{2,1,0:T(8,128)(2,1)} %l_hbm.1, bf16[1,32,1024]{2,1,0:T(8,128)(2,1)} %theta_ref.1, f32[1]{0:T(128)S(6)} %copy.5.weight_ref), custom_call_target="tpu_custom_call" | custom-call | tf_op jit(solution)/shard_map/pallas_call | solution.py:167
  43.6 1.5 %copy.6 = f32[16,1024]{1,0:T(8,128)} copy(f32[16,1024]{1,0:T(8,128)} %shard_map.37) | data formatting | bytes 131072

commit v2 on v1

v2 whole, which is shorter than its diff:
```python
import functools

import jax
import jax.numpy as jnp
from jax import lax
from jax.experimental import pallas as pl
from jax.experimental.pallas import tpu as pltpu
from jax.sharding import PartitionSpec as P

MESH = pl.DeviceIdType.MESH
NT = (((1,), (1,)), ((), ()))


def exchange_kernel(
    sizes, l_hbm, theta_hbm, weight_ref, out_ref,
    lv, th, wbuf, own, sbuf, rbuf, fsend, frecv,
    l_sem, w_sem, z_send, y_send, c_send, th_recv, x_send, x_recv, f_send, f_recv,
):
    n_chol, vectors, occupied, block_rows = sizes
    n_hi = n_chol // 2
    half = occupied // 2
    chunk_rows = 2 * block_rows
    n_chunks = n_hi
    n_groups = n_hi // 2
    w = lax.axis_index("walker")
    s = lax.axis_index("slab")
    me = lax.axis_index("chol")
    z, y = me // 2, me % 2
    step = 1 - 2 * (z % 2)
    sibling = {"walker": 1 - w}
    peer = {"slab": 1 - s}
    y_peer = {"chol": z * 2 + 1 - y}

    def line(at):
        return jnp.logical_and(at >= 0, at < n_hi)

    def signal(to):
        pl.semaphore_signal(barrier, inc=1, device_id=to, device_id_type=MESH)

    barrier = pltpu.get_barrier_semaphore()
    signal(sibling)
    signal(y_peer)
    signal({"chol": (z + step) * 2 + y})
    signal(peer)

    @pl.when(line(z - step))
    def _():
        signal({"chol": (z - step) * 2 + y})

    mine = pl.ds(pl.multiple_of(w * half, half), half)
    other = pl.ds(pl.multiple_of((1 - w) * half, half), half)
    keep = pltpu.make_async_copy(theta_hbm.at[0], th.at[w, me], l_sem.at[2])
    load_mine = pltpu.make_async_copy(l_hbm.at[:, mine], lv.at[:, mine], l_sem.at[0])
    load_other = pltpu.make_async_copy(l_hbm.at[:, other], lv.at[:, other], l_sem.at[1])
    keep.start()
    wbuf[w] = jnp.full(wbuf.shape[1:], weight_ref[0], jnp.float32)
    keep.wait()

    pl.semaphore_wait(barrier, 4 + line(z - step).astype(jnp.int32))

    def rdma(src, dst, send, recv, to):
        return pltpu.make_async_remote_copy(
            src_ref=src, dst_ref=dst, send_sem=send, recv_sem=recv, device_id=to, device_id_type=MESH
        )

    def pass_on(block, sem, to):
        return rdma(th.at[w, block], th.at[w, block], sem.at[block], th_recv.at[w, block], to)

    def arrived(walker, block):
        rdma(th.at[walker, block], th.at[walker, block], c_send.at[0], th_recv.at[walker, block], sibling).wait_recv()

    def relay(block, onward):
        @pl.when(line(onward))
        def _():
            pass_on(block, z_send, {"chol": onward * 2 + y}).start()

        pass_on(block, y_send, y_peer).start()
        pass_on(block, c_send, sibling).start()

    def from_line(d, way):
        at = z + way * d

        @pl.when(line(at))
        def _():
            arrived(w, at * 2 + y)
            relay(at * 2 + y, z - way)

    def from_y(at):
        @pl.when(line(at))
        def _():
            arrived(w, at * 2 + 1 - y)
            pass_on(at * 2 + 1 - y, c_send, sibling).start()

    @pl.when(line(z - step))
    def _():
        rdma(th.at[w, me], th.at[w, me], z_send.at[n_chol], th_recv.at[w, me], {"chol": (z - step) * 2 + y}).start()

    relay(me, z + step)
    weights = rdma(wbuf.at[w], wbuf.at[w], w_sem.at[0], w_sem.at[1], sibling)
    weights.start()
    load_mine.start()
    load_other.start()
    from_line(1, step)
    from_line(1, -step)
    from_y(z)
    from_y(z + step)
    from_line(2, step)
    from_line(2, -step)

    def margins(t, q):
        at = lax.rem(z + 1 + t, n_hi)
        rows = pl.ds(pl.multiple_of(w * half + at * chunk_rows, chunk_rows), chunk_rows)
        x = lv[:, rows, :].reshape(vectors * chunk_rows, -1)
        theta = th[:, pl.ds(4 * q, 4)]
        width = 4 * theta.shape[2]
        both = lax.dot_general(
            x, theta.reshape(2 * width, -1), NT, preferred_element_type=jnp.float32
        )
        a = wbuf[0][:1, :1] * both[:, :width] + wbuf[1][:1, :1] * both[:, width:]
        own[t, q] = a
        sbuf[t, q] = a.astype(jnp.bfloat16)
        rdma(sbuf.at[t, q], rbuf.at[t, q], x_send.at[t, q], x_recv.at[t, q], peer).start()

    def group_arrived(q):
        for k in range(4):
            arrived(1 - w, 4 * q + k)

    def some_margins(first, last, q):
        def body(t, carry):
            margins(t, q)
            return carry

        lax.fori_loop(first, last, body, 0)

    here = z // 2
    group_arrived(here)
    rdma(wbuf.at[1 - w], wbuf.at[1 - w], w_sem.at[0], w_sem.at[1], sibling).wait_recv()
    load_mine.wait()
    some_margins(0, n_chunks - 1, here)
    for d in range(3, n_hi):
        from_line(d, step)
        from_line(d, -step)
    from_y(z - step)
    for d in range(2, n_hi):
        from_y(z + d * step)
        from_y(z - d * step)
    for k in range(1, n_groups):
        q = lax.rem(here + k, n_groups)
        group_arrived(q)
        some_margins(0, n_chunks - 1, q)
    for k in range(n_groups):
        some_margins(n_chunks - 1, n_chunks, lax.rem(here + k, n_groups))
    load_other.wait()

    def fock(t, carry):
        at = lax.rem(z + 1 + t, n_hi)
        totals = []
        for q in range(n_groups):
            rdma(sbuf.at[t, q], rbuf.at[t, q], x_send.at[t, q], x_recv.at[t, q], peer).wait_recv()
        for q in range(n_groups):
            totals.append(own[t, q] + rbuf[t, q].astype(jnp.float32))
        total = jnp.concatenate(
            [
                total[g * chunk_rows : (g + 1) * chunk_rows]
                for g in range(vectors)
                for total in totals
            ],
            axis=1,
        )
        high = total.astype(jnp.bfloat16)
        low = (total - high.astype(jnp.float32)).astype(jnp.bfloat16)
        both = jnp.dot(
            jnp.concatenate([high, low], axis=0),
            lv[...].reshape(vectors * occupied, -1),
            preferred_element_type=jnp.float32,
        )
        f = both[:chunk_rows] + both[chunk_rows:]
        for d in range(2):
            fsend[t, d] = f[d * block_rows : (d + 1) * block_rows]
            to = at * 2 + d

            @pl.when(to != me)
            def _():
                rdma(fsend.at[t, d], frecv.at[me], f_send.at[t, d], f_recv.at[me], {"chol": to}).start()

        return carry

    lax.fori_loop(0, n_chunks, fock, 0)

    result = fsend[n_chunks - 1, y]
    for k in range(1, n_chol):
        source = lax.rem(me + k, n_chol)
        rdma(frecv.at[source], frecv.at[source], f_send.at[0, 0], f_recv.at[source], sibling).wait_recv()
        result = result + frecv[source]
    out_ref[...] = result

    weights.wait_send()

    @pl.when(line(z - step))
    def _():
        rdma(th.at[w, me], th.at[w, me], z_send.at[n_chol], th_recv.at[w, me], peer).wait_send()

    pass_on(me, z_send, peer).wait_send()

    def drain_theta(at, carry):
        for d in range(2):
            pass_on(at * 2 + d, c_send, sibling).wait_send()
        pass_on(at * 2 + y, y_send, peer).wait_send()
        onward = jnp.where(at > z, z - 1, z + 1)

        @pl.when(jnp.logical_and(at != z, line(onward)))
        def _():
            pass_on(at * 2 + y, z_send, peer).wait_send()

        return carry

    lax.fori_loop(0, n_hi, drain_theta, 0)

    def drain(t, carry):
        at = lax.rem(z + 1 + t, n_hi)
        for q in range(n_groups):
            rdma(sbuf.at[t, q], rbuf.at[t, q], x_send.at[t, q], x_recv.at[t, q], peer).wait_send()
        for d in range(2):

            @pl.when(at * 2 + d != me)
            def _():
                rdma(fsend.at[t, d], frecv.at[me], f_send.at[t, d], f_recv.at[me], peer).wait_send()

        return carry

    lax.fori_loop(0, n_chunks, drain, 0)


def fused(n_chol, cholesky_factors, greens, walker_weights):
    vectors, occupied, orbitals = cholesky_factors.shape
    theta_rows = greens.shape[1]
    block_rows = occupied // (2 * n_chol)
    n_hi = n_chol // 2
    n_groups = n_hi // 2
    rows = vectors * 2 * block_rows
    width = 4 * theta_rows
    dma = pltpu.SemaphoreType.DMA
    return pl.pallas_call(
        functools.partial(exchange_kernel, (n_chol, vectors, occupied, block_rows)),
        out_shape=jax.ShapeDtypeStruct((block_rows, orbitals), jnp.float32),
        in_specs=[
            pl.BlockSpec(memory_space=pl.ANY),
            pl.BlockSpec(memory_space=pl.ANY),
            pl.BlockSpec(memory_space=pltpu.SMEM),
        ],
        out_specs=pl.BlockSpec(memory_space=pltpu.VMEM),
        scratch_shapes=[
            pltpu.VMEM((vectors, occupied, orbitals), jnp.bfloat16),
            pltpu.VMEM((2, n_chol, theta_rows, orbitals), jnp.bfloat16),
            pltpu.VMEM((2, 8, 128), jnp.float32),
            pltpu.VMEM((n_hi, n_groups, rows, width), jnp.float32),
            pltpu.VMEM((n_hi, n_groups, rows, width), jnp.bfloat16),
            pltpu.VMEM((n_hi, n_groups, rows, width), jnp.bfloat16),
            pltpu.VMEM((n_hi, 2, block_rows, orbitals), jnp.float32),
            pltpu.VMEM((n_chol, block_rows, orbitals), jnp.float32),
            dma((3,)),
            dma((2,)),
            dma((n_chol + 1,)),
            dma((n_chol,)),
            dma((n_chol,)),
            dma((2, n_chol)),
            dma((n_hi, n_groups)),
            dma((n_hi, n_groups)),
            dma((n_hi, 2)),
            dma((n_chol,)),
        ],
        compiler_params=pltpu.CompilerParams(collective_id=0, has_side_effects=True),
    )(cholesky_factors, greens, walker_weights)


def plain(cholesky_factors, greens, walker_weights):
    panel_sum_terms = jnp.einsum(
        "gnp,mp->gnm",
        cholesky_factors,
        lax.all_gather(greens[0], "chol", axis=0, tiled=True),
        preferred_element_type=jnp.float32,
    )
    margin = lax.psum(panel_sum_terms, "slab").astype(jnp.bfloat16)
    terms = jnp.einsum("gnm,gmp->np", margin, cholesky_factors, preferred_element_type=jnp.float32)
    weighted = walker_weights[0] * terms
    return lax.psum_scatter(weighted, ("walker", "chol"), scatter_dimension=0, tiled=True)


def solution(mesh):
    walkers, slabs, n_chol = (mesh.shape[axis] for axis in ("walker", "slab", "chol"))

    def per_device(cholesky_factors, greens, walker_weights):
        occupied = cholesky_factors.shape[1]
        pair = walkers == 2 and slabs == 2 and greens.shape[0] == 1
        fits = n_chol % 4 == 0 and occupied % (16 * n_chol) == 0 and 4 * greens.shape[1] % 128 == 0
        if pair and fits:
            return fused(n_chol, cholesky_factors, greens, walker_weights)
        return plain(cholesky_factors, greens, walker_weights)

    in_specs = (P("chol", None, "slab"), P("walker", "chol", "slab"), P("walker"))
    out_specs = P(("walker", "chol"), "slab")
    return jax.shard_map(
        per_device, mesh=mesh, in_specs=in_specs, out_specs=out_specs, check_vma=False
    )
```

time: 45.3 us -> 40.2 us (0.89)
  Pallas kernels: 42.9 us -> 37.6 us
    pallas_call x1, Pallas kernels: 42.9 us -> 37.6 us  [fused(): pl.pallas_call(functools.partial(exchange_kernel, (n_chol, vectors, occup...]
where the time goes in v2:
time: 40.2 us; the launch traced here: 39.8 us
  Pallas kernels  37.6 us (94%)
  local copies, waits for them, and re-layouts  1.47 us (4%)
  between operations  0.66 us (2%)
    pallas_call x1, Pallas kernels, fused(): pl.pallas_call(functools.partial(exchange_kernel, (n_chol, vectors, occup...  37.6 us
    unnamed x1, local copies, waits for them, and re-layouts  1.47 us

profile of v2, /device:TPU:0, one launch (start us, length us, event | category | flops | bytes accessed | tf_op | source)
XLA Modules:
  0.0 39.8 jit_solution(15667065993505519563)
XLA Ops:
  0.7 37.6 %shard_map.37 = f32[16,1024]{1,0:T(8,128)} custom-call(bf16[12,256,1024]{2,1,0:T(8,128)(2,1)} %l_hbm.1, bf16[1,32,1024]{2,1,0:T(8,128)(2,1)} %theta_hbm.1, f32[1]{0:T(128)S(6)} %copy.5.weight_ref), custom_call_target="tpu_custom_call" | custom-call | tf_op jit(solution)/shard_map/pallas_call | solution.py:243
  38.3 1.5 %copy.6 = f32[16,1024]{1,0:T(8,128)} copy(f32[16,1024]{1,0:T(8,128)} %shard_map.37) | data formatting | bytes 131072

commit v3 on v2

--- a/solution.py
+++ b/solution.py
@@ -13,8 +13,8 @@
 
 def exchange_kernel(
     sizes, l_hbm, theta_hbm, weight_ref, out_ref,
-    lv, th, wbuf, own, sbuf, rbuf, fsend, frecv,
-    l_sem, w_sem, z_send, y_send, c_send, th_recv, x_send, x_recv, f_send, f_recv,
+    lv, th, wbuf, own, sbuf, rbuf, own_small, sbuf_small, rbuf_small, fsend, frecv, yrecv,
+    l_sem, w_sem, z_send, y_send, c_send, th_recv, x_send, x_recv, f_send, f_recv, fy_send, fy_recv,
 ):
     n_chol, vectors, occupied, block_rows = sizes
     n_hi = n_chol // 2
@@ -31,6 +31,10 @@
     peer = {"slab": 1 - s}
     y_peer = {"chol": z * 2 + 1 - y}
 
+    def partner(t):
+        k = n_hi - 1 - t
+        return lax.rem(z // 2 + k // 2, n_groups) * 2 + lax.rem(z + k, 2)
+
     def line(at):
         return jnp.logical_and(at >= 0, at < n_hi)
 
@@ -107,36 +111,58 @@
     from_line(2, step)
     from_line(2, -step)
 
-    def margins(t, q):
-        at = lax.rem(z + 1 + t, n_hi)
-        rows = pl.ds(pl.multiple_of(w * half + at * chunk_rows, chunk_rows), chunk_rows)
-        x = lv[:, rows, :].reshape(vectors * chunk_rows, -1)
+    def slots(unit, q):
+        if isinstance(unit, tuple):
+            at, to = (unit[1], q), (n_chunks - 1 + unit[1], q)
+            bufs = own_small.at[at], sbuf_small.at[at], rbuf_small.at[at]
+        else:
+            at = to = (unit, q)
+            bufs = own.at[at], sbuf.at[at], rbuf.at[at]
+        return bufs + (rdma(bufs[1], bufs[2], x_send.at[to], x_recv.at[to], peer),)
+
+    def margins(unit, q):
+        if isinstance(unit, tuple):
+            count = block_rows
+            start = z * chunk_rows + jnp.where(unit[1] == 0, 1 - y, y) * block_rows
+        else:
+            count = chunk_rows
+            start = partner(unit) * chunk_rows
+        rows = pl.ds(pl.multiple_of(w * half + start, count), count)
+        x = lv[:, rows, :].reshape(vectors * count, -1)
         theta = th[:, pl.ds(4 * q, 4)]
         width = 4 * theta.shape[2]
         both = lax.dot_general(
             x, theta.reshape(2 * width, -1), NT, preferred_element_type=jnp.float32
         )
         a = wbuf[0][:1, :1] * both[:, :width] + wbuf[1][:1, :1] * both[:, width:]
-        own[t, q] = a
-        sbuf[t, q] = a.astype(jnp.bfloat16)
-        rdma(sbuf.at[t, q], rbuf.at[t, q], x_send.at[t, q], x_recv.at[t, q], peer).start()
+        keep_ref, send_ref, _, copy = slots(unit, q)
+        keep_ref[...] = a
+        send_ref[...] = a.astype(jnp.bfloat16)
+        copy.start()
 
     def group_arrived(q):
         for k in range(4):
             arrived(1 - w, 4 * q + k)
 
-    def some_margins(first, last, q):
+    def big_margins(q):
         def body(t, carry):
             margins(t, q)
             return carry
 
-        lax.fori_loop(first, last, body, 0)
+        lax.fori_loop(0, n_chunks - 1, body, 0)
+
+    def small_margins(q):
+        def body(i, carry):
+            margins((None, i), q)
+            return carry
+
+        lax.fori_loop(0, 2, body, 0)
 
     here = z // 2
     group_arrived(here)
     rdma(wbuf.at[1 - w], wbuf.at[1 - w], w_sem.at[0], w_sem.at[1], sibling).wait_recv()
     load_mine.wait()
-    some_margins(0, n_chunks - 1, here)
+    big_margins(here)
     for d in range(3, n_hi):
         from_line(d, step)
         from_line(d, -step)
@@ -147,51 +173,86 @@
     for k in range(1, n_groups):
         q = lax.rem(here + k, n_groups)
         group_arrived(q)
-        some_margins(0, n_chunks - 1, q)
+        big_margins(q)
     for k in range(n_groups):
-        some_margins(n_chunks - 1, n_chunks, lax.rem(here + k, n_groups))
+        small_margins(lax.rem(here + k, n_groups))
     load_other.wait()
 
-    def fock(t, carry):
-        at = lax.rem(z + 1 + t, n_hi)
-        totals = []
-        for q in range(n_groups):
-            rdma(sbuf.at[t, q], rbuf.at[t, q], x_send.at[t, q], x_recv.at[t, q], peer).wait_recv()
-        for q in range(n_groups):
-            totals.append(own[t, q] + rbuf[t, q].astype(jnp.float32))
+    def fock(unit, q):
+        keep_ref, _, got_ref, copy = slots(unit, q)
+        copy.wait_recv()
+        total = keep_ref[...] + got_ref[...].astype(jnp.float32)
+        count, width = total.shape[0] // vectors, total.shape[1]
         total = jnp.concatenate(
-            [
-                total[g * chunk_rows : (g + 1) * chunk_rows]
-                for g in range(vectors)
-                for total in totals
-            ],
-            axis=1,
+            [total[g * count : (g + 1) * count] for g in range(vectors)], axis=1
         )
         high = total.astype(jnp.bfloat16)
         low = (total - high.astype(jnp.float32)).astype(jnp.bfloat16)
+        m = pl.ds(pl.multiple_of(q * width, width), width)
         both = jnp.dot(
             jnp.concatenate([high, low], axis=0),
-            lv[...].reshape(vectors * occupied, -1),
+            lv[:, m, :].reshape(vectors * width, -1),
             preferred_element_type=jnp.float32,
         )
-        f = both[:chunk_rows] + both[chunk_rows:]
-        for d in range(2):
-            fsend[t, d] = f[d * block_rows : (d + 1) * block_rows]
-            to = at * 2 + d
-
-            @pl.when(to != me)
-            def _():
-                rdma(fsend.at[t, d], frecv.at[me], f_send.at[t, d], f_recv.at[me], {"chol": to}).start()
-
-        return carry
-
-    lax.fori_loop(0, n_chunks, fock, 0)
-
-    result = fsend[n_chunks - 1, y]
-    for k in range(1, n_chol):
-        source = lax.rem(me + k, n_chol)
-        rdma(frecv.at[source], frecv.at[source], f_send.at[0, 0], f_recv.at[source], sibling).wait_recv()
+        return both[:count] + both[count:]
+
+    def to_y(t, d):
+        return rdma(fsend.at[t, d], yrecv.at[t], fy_send.at[t], fy_recv.at[t], y_peer)
+
+    def along_z(t):
+        to = {"chol": partner(t) * 2 + y}
+        return rdma(fsend.at[t, y], frecv.at[z], f_send.at[t], f_recv.at[z], to)
+
+    def add_and_pass(t):
+        to_y(t, 1 - y).wait_recv()
+        fsend[t, y] = fsend[t, y] + yrecv[t]
+        along_z(t).start()
+
+    for k in range(n_groups):
+        q = lax.rem(here + k, n_groups)
+        first, last = k == 0, k == n_groups - 1
+
+        def big(t, carry):
+            f = fock(t, q)
+            for d in range(2):
+                rows = f[d * block_rows : (d + 1) * block_rows]
+                fsend[t, d] = rows if first else fsend[t, d] + rows
+            if last:
+                to_y(t, 1 - y).start()
+
+                @pl.when(t > 0)
+                def _():
+                    add_and_pass(t - 1)
+
+            return carry
+
+        lax.fori_loop(0, n_chunks - 1, big, 0)
+
+    for k in range(n_groups):
+        q = lax.rem(here + k, n_groups)
+        first, last = k == 0, k == n_groups - 1
+
+        def small(i, carry):
+            rows = fock((None, i), q)
+            fsend[n_chunks - 1, i] = rows if first else fsend[n_chunks - 1, i] + rows
+            if last:
+
+                @pl.when(i == 0)
+                def _():
+                    to_y(n_chunks - 1, 0).start()
+                    add_and_pass(n_chunks - 2)
+
+            return carry
+
+        lax.fori_loop(0, 2, small, 0)
+
+    result = fsend[n_chunks - 1, 1]
+    for k in range(1, n_hi):
+        source = lax.rem(z + k, n_hi)
+        rdma(frecv.at[source], frecv.at[source], f_send.at[0], f_recv.at[source], sibling).wait_recv()
         result = result + frecv[source]
+    to_y(n_chunks - 1, 0).wait_recv()
+    result = result + yrecv[n_chunks - 1]
     out_ref[...] = result
 
     weights.wait_send()
@@ -217,18 +278,17 @@
     lax.fori_loop(0, n_hi, drain_theta, 0)
 
     def drain(t, carry):
-        at = lax.rem(z + 1 + t, n_hi)
         for q in range(n_groups):
-            rdma(sbuf.at[t, q], rbuf.at[t, q], x_send.at[t, q], x_recv.at[t, q], peer).wait_send()
-        for d in range(2):
-
-            @pl.when(at * 2 + d != me)
-            def _():
-                rdma(fsend.at[t, d], frecv.at[me], f_send.at[t, d], f_recv.at[me], peer).wait_send()
-
+            slots(t, q)[3].wait_send()
+        to_y(t, 1 - y).wait_send()
+        along_z(t).wait_send()
         return carry
 
-    lax.fori_loop(0, n_chunks, drain, 0)
+    lax.fori_loop(0, n_chunks - 1, drain, 0)
+    for i in range(2):
+        for q in range(n_groups):
+            slots((None, i), q)[3].wait_send()
+    to_y(n_chunks - 1, 0).wait_send()
 
 
 def fused(n_chol, cholesky_factors, greens, walker_weights):
@@ -253,21 +313,27 @@
             pltpu.VMEM((vectors, occupied, orbitals), jnp.bfloat16),
             pltpu.VMEM((2, n_chol, theta_rows, orbitals), jnp.bfloat16),
             pltpu.VMEM((2, 8, 128), jnp.float32),
-            pltpu.VMEM((n_hi, n_groups, rows, width), jnp.float32),
-            pltpu.VMEM((n_hi, n_groups, rows, width), jnp.bfloat16),
-            pltpu.VMEM((n_hi, n_groups, rows, width), jnp.bfloat16),
+            pltpu.VMEM((n_hi - 1, n_groups, rows, width), jnp.float32),
+            pltpu.VMEM((n_hi - 1, n_groups, rows, width), jnp.bfloat16),
+            pltpu.VMEM((n_hi - 1, n_groups, rows, width), jnp.bfloat16),
+            pltpu.VMEM((2, n_groups, rows // 2, width), jnp.float32),
+            pltpu.VMEM((2, n_groups, rows // 2, width), jnp.bfloat16),
+            pltpu.VMEM((2, n_groups, rows // 2, width), jnp.bfloat16),
             pltpu.VMEM((n_hi, 2, block_rows, orbitals), jnp.float32),
-            pltpu.VMEM((n_chol, block_rows, orbitals), jnp.float32),
+            pltpu.VMEM((n_hi, block_rows, orbitals), jnp.float32),
+            pltpu.VMEM((n_hi, block_rows, orbitals), jnp.float32),
             dma((3,)),
             dma((2,)),
             dma((n_chol + 1,)),
             dma((n_chol,)),
             dma((n_chol,)),
             dma((2, n_chol)),
-            dma((n_hi, n_groups)),
-            dma((n_hi, n_groups)),
-            dma((n_hi, 2)),
-            dma((n_chol,)),
+            dma((n_hi + 1, n_groups)),
+            dma((n_hi + 1, n_groups)),
+            dma((n_hi,)),
+            dma((n_hi,)),
+            dma((n_hi,)),
+            dma((n_hi,)),
         ],
         compiler_params=pltpu.CompilerParams(collective_id=0, has_side_effects=True),
     )(cholesky_factors, greens, walker_weights)

time: 40.2 us -> 39.8 us (0.990)
  no operation moved by 1% of the time
where the time goes in v3:
time: 39.8 us; the launch traced here: 39.6 us
  Pallas kernels  37.4 us (94%)
  local copies, waits for them, and re-layouts  1.47 us (4%)
  between operations  0.66 us (2%)
    pallas_call x1, Pallas kernels, fused(): pl.pallas_call(functools.partial(exchange_kernel, (n_chol, vectors, occup...  37.4 us
    unnamed x1, local copies, waits for them, and re-layouts  1.47 us

profile of v3, /device:TPU:0, one launch (start us, length us, event | category | flops | bytes accessed | tf_op | source)
XLA Modules:
  0.0 39.6 jit_solution(9140664785896271879)
XLA Ops:
  0.7 37.4 %shard_map.37 = f32[16,1024]{1,0:T(8,128)} custom-call(bf16[12,256,1024]{2,1,0:T(8,128)(2,1)} %l_hbm.1, bf16[1,32,1024]{2,1,0:T(8,128)(2,1)} %theta_hbm.1, f32[1]{0:T(128)S(6)} %copy.5.weight_ref), custom_call_target="tpu_custom_call" | custom-call | tf_op jit(solution)/shard_map/pallas_call | solution.py:303
  38.1 1.5 %copy.6 = f32[16,1024]{1,0:T(8,128)} copy(f32[16,1024]{1,0:T(8,128)} %shard_map.37) | data formatting | bytes 131072

commit v4 on v3

--- a/solution.py
+++ b/solution.py
@@ -197,7 +197,8 @@
         return both[:count] + both[count:]
 
     def to_y(t, d):
-        return rdma(fsend.at[t, d], yrecv.at[t], fy_send.at[t], fy_recv.at[t], y_peer)
+        to = {"chol": jnp.where(t == n_chunks - 2, partner(t), z) * 2 + 1 - y}
+        return rdma(fsend.at[t, d], yrecv.at[t], fy_send.at[t], fy_recv.at[t], to)
 
     def along_z(t):
         to = {"chol": partner(t) * 2 + y}
@@ -220,6 +221,10 @@
             if last:
                 to_y(t, 1 - y).start()
 
+                @pl.when(t == n_chunks - 2)
+                def _():
+                    along_z(t).start()
+
                 @pl.when(t > 0)
                 def _():
                     add_and_pass(t - 1)
@@ -240,7 +245,6 @@
                 @pl.when(i == 0)
                 def _():
                     to_y(n_chunks - 1, 0).start()
-                    add_and_pass(n_chunks - 2)
 
             return carry
 
@@ -251,8 +255,9 @@
         source = lax.rem(z + k, n_hi)
         rdma(frecv.at[source], frecv.at[source], f_send.at[0], f_recv.at[source], sibling).wait_recv()
         result = result + frecv[source]
-    to_y(n_chunks - 1, 0).wait_recv()
-    result = result + yrecv[n_chunks - 1]
+    for t in (n_chunks - 2, n_chunks - 1):
+        to_y(t, 0).wait_recv()
+        result = result + yrecv[t]
     out_ref[...] = result
 
     weights.wait_send()

time: 39.8 us -> 38.7 us (0.972)
  Pallas kernels: 37.4 us -> 36.4 us
    pallas_call x1, Pallas kernels: 37.4 us -> 36.4 us  [fused(): pl.pallas_call(functools.partial(exchange_kernel, (n_chol, vectors, occup...]
where the time goes in v4:
time: 38.7 us; the launch traced here: 38.5 us
  Pallas kernels  36.4 us (94%)
  local copies, waits for them, and re-layouts  1.47 us (4%)
  between operations  0.66 us (2%)
    pallas_call x1, Pallas kernels, fused(): pl.pallas_call(functools.partial(exchange_kernel, (n_chol, vectors, occup...  36.4 us
    unnamed x1, local copies, waits for them, and re-layouts  1.47 us

profile of v4, /device:TPU:0, one launch (start us, length us, event | category | flops | bytes accessed | tf_op | source)
XLA Modules:
  0.0 38.5 jit_solution(7473421951872927667)
XLA Ops:
  0.7 36.4 %shard_map.37 = f32[16,1024]{1,0:T(8,128)} custom-call(bf16[12,256,1024]{2,1,0:T(8,128)(2,1)} %l_hbm.1, bf16[1,32,1024]{2,1,0:T(8,128)(2,1)} %theta_hbm.1, f32[1]{0:T(128)S(6)} %copy.5.weight_ref), custom_call_target="tpu_custom_call" | custom-call | tf_op jit(solution)/shard_map/pallas_call | solution.py:308
  37.1 1.5 %copy.6 = f32[16,1024]{1,0:T(8,128)} copy(f32[16,1024]{1,0:T(8,128)} %shard_map.37) | data formatting | bytes 131072
